TPU v7x, 32 devices: a whole 2x2x4 slice. The times are simulated.
32 devices in a mesh: group: 4 (over x, core), tensor: 4 (over z), dp: 2 (over y).
Axes of the slice: x: 2, y: 2, z: 4, core: 2. Of those that a mesh axis runs over, the one named last changes fastest.
Arguments:
- doc_emb: bfloat16 [48, 4096], P('group', 'dp'), may hold values from -6 to 6
- row_emb: bfloat16 [64, 4096], P(None, 'dp'), may hold values from -6 to 6
- hyper_in: bfloat16 [4096, 8192], P('dp', 'tensor'), may hold values from -0.09375 to 0.09375
- hyper_out: bfloat16 [8192, 8192], P('tensor', 'dp'), may hold values from -0.0625 to 0.0625
- assign: int32 [48], replicated, may hold values from 0 to 47, each once
- states: bfloat16 [2304, 8192], P('group', 'tensor'), may hold values from -6 to 6
- proj_weight: bfloat16 [8192, 8192], P('tensor', 'dp'), may hold values from -0.0625 to 0.0625
- targets: bfloat16 [2304, 8192], P(('group', 'tensor'), 'dp'), may hold values from -6 to 6
Outputs:
- adapted: bfloat16 [2304, 8192], P(('group', 'tensor'), 'dp')
- grad_down: float32 [48, 32, 8192], P('group', None, 'tensor')
- grad_up: float32 [48, 32, 8192], P('group', None, ('dp', 'tensor'))
Inputs may be any that keep to these rules, and one draw needn't show every extreme that they name: `assign`: every document is named by exactly one slot.
All inputs are finite; a program needn't handle non-finite values.
Results may differ from a plain program's by a relative error of at most 0.02.
Values may be sent and summed in bfloat16 or wider, within the bound.
No kernel may reach another device: no remote copies, remote signals or barrier semaphores. Data moves between devices by JAX's collectives and lax.ppermute only.
A program may use at most 128 MiB of HBM per device.

v0:
```python
import math

import jax
import jax.numpy as jnp
from jax import lax
from jax.sharding import PartitionSpec as P

D = 8192
R = 32


LOWDIM_MULTIPLE = 0.1


def spread(block, axis, owner):
    block = jnp.where(lax.axis_index(axis) == owner, block, jnp.zeros_like(block))
    return lax.psum(block, axis)


def hypernet(doc_rows, row_emb, hyper_in, hyper_out):
    doc_count = doc_rows.shape[0]
    pre_doc, pre_row = (
        lax.psum(
            jnp.dot(doc_rows, hyper_in, preferred_element_type=jnp.float32).astype(jnp.bfloat16),
            "dp",
        ).astype(jnp.float32),
        lax.psum(
            jnp.dot(row_emb, hyper_in, preferred_element_type=jnp.float32).astype(jnp.bfloat16),
            "dp",
        ).astype(jnp.float32),
    )
    hidden = jax.nn.silu(pre_doc[:, None, :] + pre_row[None, :, :]).astype(jnp.bfloat16)
    hidden = hidden.reshape(doc_count * 2 * R, hidden.shape[2])
    partial_value = jnp.dot(hidden, hyper_out, preferred_element_type=jnp.float32)
    summed = lax.psum(partial_value.astype(jnp.bfloat16), "tensor")
    factors = summed.reshape(doc_count, 2 * R, hyper_out.shape[1])
    ratio_axes = lax.axis_size("tensor") // lax.axis_size("dp")
    owner_rows = spread(factors[:, :R, :], "dp", lax.axis_index("tensor") // ratio_axes)
    col_width = hyper_out.shape[1] // ratio_axes
    down_block = lax.dynamic_slice_in_dim(
        owner_rows, lax.axis_index("tensor") % ratio_axes * col_width, col_width, 2
    )
    return (down_block, factors[:, R:, :])


def body(doc_emb, row_emb, hyper_in, hyper_out, assign, states, proj_weight, targets):
    doc_count = doc_emb.shape[0]
    group_start = lax.axis_index("group") * doc_count
    slot_docs = lax.dynamic_slice_in_dim(assign, group_start, doc_count)
    everyone = lax.all_gather(doc_emb, "group", axis=0, tiled=True)
    picker = (slot_docs[:, None] == jnp.arange(everyone.shape[0], dtype=jnp.int32)[None, :]).astype(
        jnp.bfloat16
    )
    chosen = jnp.dot(picker, everyone, preferred_element_type=jnp.float32).astype(jnp.bfloat16)
    slot_down, slot_up_factor = hypernet(chosen, row_emb, hyper_in, hyper_out)
    token_count = states.shape[0]
    per_doc = token_count // doc_count
    fan_width_multiplier = 1.0 / math.sqrt(D)
    bundled_entries = states.reshape(doc_count, per_doc, states.shape[1])
    low_part = jnp.einsum(
        "quw,qlw->qul", bundled_entries, slot_down, preferred_element_type=jnp.float32
    ).reshape(token_count, R)
    base_part = jnp.dot(states, proj_weight, preferred_element_type=jnp.float32)
    frozen_output, low_sum = (
        lax.psum_scatter(
            base_part.astype(jnp.bfloat16), "tensor", scatter_dimension=0, tiled=True
        ).astype(jnp.float32),
        lax.psum_scatter(
            low_part.astype(jnp.bfloat16), "tensor", scatter_dimension=0, tiled=True
        ).astype(jnp.float32),
    )
    row_count = frozen_output.shape[0]
    row_start = lax.axis_index("tensor") * row_count
    owner_doc = (row_start + jnp.arange(row_count, dtype=jnp.int32)) // per_doc
    document_member = owner_doc[:, None] == jnp.arange(doc_count, dtype=jnp.int32)[None, :]
    narrow_basis_map = (low_sum * fan_width_multiplier).astype(jnp.bfloat16)
    broadcast_rows = jnp.where(
        document_member[:, :, None], narrow_basis_map[:, None, :], jnp.zeros((), jnp.bfloat16)
    ).reshape(row_count, doc_count * R)
    up_factor_rows = slot_up_factor.reshape(doc_count * R, slot_up_factor.shape[2])
    raised_rows = frozen_output + LOWDIM_MULTIPLE * jnp.dot(
        broadcast_rows, up_factor_rows, preferred_element_type=jnp.float32
    )
    adapted = raised_rows.astype(jnp.bfloat16)
    residual = (raised_rows - targets.astype(jnp.float32)).astype(jnp.bfloat16)
    partial_up_gradient = LOWDIM_MULTIPLE * lax.dot_general(
        broadcast_rows, residual, (((0,), (0,)), ((), ())), preferred_element_type=jnp.float32
    )
    grad_up_local = lax.psum_scatter(
        partial_up_gradient.reshape(doc_count, R, up_factor_rows.shape[1]).astype(jnp.bfloat16),
        "tensor",
        scatter_dimension=2,
        tiled=True,
    ).astype(jnp.float32)
    document_list = lax.dot_general(
        residual, up_factor_rows, (((1,), (1,)), ((), ())), preferred_element_type=jnp.float32
    ).reshape(row_count, doc_count, R)
    token_portion = LOWDIM_MULTIPLE * jnp.sum(
        jnp.where(document_member[:, :, None], document_list, 0.0), axis=1
    )
    placed = lax.dynamic_update_slice_in_dim(
        jnp.zeros((token_count, R), jnp.float32), token_portion, row_start, 0
    )
    position_sensitivity = lax.psum(placed, ("tensor", "dp")).astype(jnp.bfloat16)
    lowering_matrix_sensitivity = fan_width_multiplier * jnp.einsum(
        "oed,oec->odc",
        position_sensitivity.reshape(doc_count, per_doc, R),
        bundled_entries,
        preferred_element_type=jnp.float32,
    )
    own_docs = group_start + jnp.arange(doc_count, dtype=jnp.int32)
    initial_grads = (
        jnp.zeros(
            (
                doc_count,
                lowering_matrix_sensitivity.shape[1] * lowering_matrix_sensitivity.shape[2],
            ),
            jnp.float32,
        ),
        jnp.zeros((doc_count, grad_up_local.shape[1] * grad_up_local.shape[2]), jnp.float32),
    )
    pieces = (
        lax.all_gather(
            lowering_matrix_sensitivity.astype(jnp.bfloat16), "group", axis=0, tiled=True
        ).astype(jnp.float32),
        lax.all_gather(grad_up_local.astype(jnp.bfloat16), "group", axis=0, tiled=True).astype(
            jnp.float32
        ),
    )
    piece_rows = pieces[0].shape[0]
    picker = (own_docs[:, None] == assign[None, :]).astype(jnp.float32)
    first = initial_grads[0] + jnp.dot(
        picker, pieces[0].reshape(piece_rows, -1), precision=lax.Precision.HIGHEST
    )
    second = initial_grads[1] + jnp.dot(
        picker, pieces[1].reshape(piece_rows, -1), precision=lax.Precision.HIGHEST
    )
    grad_down = first.reshape(lowering_matrix_sensitivity.shape)
    grad_up = second.reshape(grad_up_local.shape)
    return (adapted, grad_down, grad_up)


def solution(mesh):
    in_specs = (
        P("group", "dp"),
        P(None, "dp"),
        P("dp", "tensor"),
        P("tensor", "dp"),
        P(),
        P("group", "tensor"),
        P("tensor", "dp"),
        P(("group", "tensor"), "dp"),
    )
    out_specs = (
        P(("group", "tensor"), "dp"),
        P("group", None, "tensor"),
        P("group", None, ("dp", "tensor")),
    )
    return jax.shard_map(body, mesh=mesh, in_specs=in_specs, out_specs=out_specs, check_vma=False)
```

profile of v0, /device:TPU:0, one launch (start us, length us, event | category | flops | bytes accessed | tf_op | source)
XLA Modules:
  0.0 643.9 jit_solution(16494009230367694234)
XLA Ops:
  7.2 0.0 copy-start
  7.2 0.0 copy-start.4
  7.2 0.0 copy-start.7
  7.2 0.0 all-reduce.4.cloned.1.call-start
  7.2 5.9 convolution_convert_fusion.2
  13.1 0.0 all-reduce.4.cloned.1.call-update
  13.2 0.0 all-reduce.6.cloned.1.call-start
  13.2 0.0 copy-done.4
  13.2 7.2 %all-gather = bf16[4,12,2048]{2,1,0:T(8,128)(2,1)S(1)} all-gather(bf16[1,12,2048]{2,1,0:T(8,128)(2,1)S(1)} %bitcast.83), channel_id=1, replica_groups=mesh['group'=4,'tensor'=4,'dp'=2] {'group'}, dimensions={0}, use_global_device_ids=true | all-gather | bytes 245760 | tf_op jit(solution)/shard_map/all_gather | solution.py:50
  20.5 0.0 copy-done.7
  20.5 0.1 dynamic_slice.6
  20.6 4.8 convolution_convert_fusion.4
  25.4 8.9 %psum.35 = bf16[12,2048]{1,0:T(8,128)(2,1)S(1)} all-reduce(bf16[12,2048]{1,0:T(8,128)(2,1)S(1)} %convolution_convert_fusion.4), channel_id=1, replica_groups=mesh['group'=4,'tensor'=4,'dp'=2] {'dp'}, use_global_device_ids=true, to_apply=%region_1.0 | all-reduce | flops 24576 | bytes 98304 | tf_op jit(solution)/shard_map/psum | solution.py:23
  34.3 5.0 all-reduce.4.cloned.1.call-done
  39.3 1.0 convert_element_type.76
  40.3 0.8 broadcast_add_fusion
  41.1 1.7 fusion.6
  42.8 18.5 %convolution_convert_fusion = bf16[768,4096]{1,0:T(8,128)(2,1)} fusion(bf16[768,2048]{1,0:T(8,128)(2,1)S(1)} %fusion.6, bf16[2048,4096]{1,0:T(8,128)(2,1)} %param.11), kind=kOutput, calls=%fused_computation | convolution fusion | flops 12888047616 | bytes 26214400 | tf_op jit(solution)/shard_map/dot_general | solution.py:34
  61.3 0.0 all-reduce.6.cloned.1.call-update
  61.4 0.0 all-reduce.8.cloned.1.call-start
  61.4 222.9 %all-reduce.6.cloned.1.call-done = bf16[12,64,4096]{2,1,0:T(8,128)(2,1)} async-done(((bf16[12,64,4096]{2,1,0:T(8,128)(2,1)}), bf16[12,64,4096]{2,1,0:T(8,128)(2,1)}) %all-reduce.6.cloned.1.call-update) | async-done | bytes 6291472 | tf_op jit(solution)/shard_map/psum | solution.py:35
  284.4 3.8 slice_select_fusion
  288.1 0.0 all-reduce.8.cloned.1.call-update
  288.1 0.0 reduce-scatter.10.cloned.1.call-start
  288.2 84.8 %all-reduce.8.cloned.1.call-done = bf16[12,32,4096]{2,1,0:T(8,128)(2,1)} async-done(((bf16[12,32,4096]{2,1,0:T(8,128)(2,1)}), bf16[12,32,4096]{2,1,0:T(8,128)(2,1)}) %all-reduce.8.cloned.1.call-update) | async-done | bytes 3145744 | tf_op jit(solution)/shard_map/psum | solution.py:17
  373.0 0.0 copy-done
  373.0 2.1 fusion.31
  375.2 0.8 copy.27
  376.0 0.0 reduce-scatter.10.cloned.1.call-update
  376.0 0.2 reduce-scatter.6.cloned.1.call-start
  376.2 15.0 %convolution_convert_fusion.1 = bf16[576,4096]{1,0:T(8,128)(2,1)} fusion(bf16[576,2048]{1,0:T(8,128)(2,1)S(1)} %copy-done, bf16[2048,4096]{1,0:T(8,128)(2,1)} %param.14), kind=kOutput, calls=%fused_computation.11 | convolution fusion | flops 9666035712 | bytes 23855104 | tf_op jit(solution)/shard_map/dot_general | solution.py:63
  391.2 0.0 reduce-scatter.6.cloned.1.call-update
  391.2 0.0 reduce-scatter.8.cloned.1.call-start
  391.3 0.0 copy-start.5
  391.3 4.4 reduce-scatter.10.cloned.1.call-done
  395.7 0.8 copy.26
  396.5 0.0 copy-done.5
  396.5 0.7 broadcast_select_fusion
  397.2 84.1 %reduce-scatter.6.cloned.1.call-done = bf16[144,4096]{1,0:T(8,128)(2,1)} async-done(((bf16[576,4096]{1,0:T(8,128)(2,1)}), bf16[144,4096]{1,0:T(8,128)(2,1)}) %reduce-scatter.6.cloned.1.call-update) | async-done | bytes 1179664 | tf_op jit(solution)/shard_map/reduce_scatter | solution.py:65
  481.4 4.1 fusion.47
  485.5 0.0 copy-done.2
  485.5 0.0 copy-done.3
  485.5 2.7 multiply_convert_fusion
  488.1 0.0 copy-done.1
  488.2 0.0 reduce-scatter.8.cloned.1.call-update
  488.2 0.0 all-gather.4.cloned.1.call-start
  488.2 0.6 copy-done.6
  488.8 3.6 fusion.23
  492.5 0.5 dynamic_update_slice.3
  492.9 40.6 %psum.39 = bf16[576,32]{0,1:T(8,128)(2,1)S(1)} all-reduce(f32[576,32]{0,1:T(8,128)S(1)} %dynamic_update_slice.3), channel_id=1, replica_groups=mesh['group'=4,'tensor'=4,'dp'=2] {'tensor','dp'}, use_global_device_ids=true, to_apply=%region_7.8 | all-reduce | flops 18432 | bytes 110592 | tf_op jit(solution)/shard_map/psum | solution.py:104
  533.5 0.2 reshape.85
  533.7 0.0 copy-start.8
  533.7 1.7 multiply_convert_fusion.1
  535.4 0.0 all-gather.4.cloned.1.call-update
  535.4 0.3 all-gather.6.cloned.1.call-start
  535.7 15.1 %reduce-scatter.8.cloned.1.call-done = bf16[12,32,1024]{2,1,0:T(8,128)(2,1)} async-done(((bf16[12,32,4096]{2,1,0:T(8,128)(2,1)}), bf16[12,32,1024]{2,1,0:T(8,128)(2,1)}) %reduce-scatter.8.cloned.1.call-update) | async-done | bytes 786448 | tf_op jit(solution)/shard_map/reduce_scatter | solution.py:89
  550.8 0.0 all-gather.6.cloned.1.call-update
  550.8 48.7 %all-gather.4.cloned.1.call-done = bf16[48,32,2048]{2,1,0:T(8,128)(2,1)} async-done(((bf16[12,32,2048]{2,1,0:T(8,128)(2,1)}), bf16[48,32,2048]{2,1,0:T(8,128)(2,1)}) %all-gather.4.cloned.1.call-update) | async-done | bytes 6291472 | tf_op jit(solution)/shard_map/all_gather | solution.py:123
  599.6 0.0 copy-done.8
  599.6 9.6 %fusion = f32[12,32,2048]{2,0,1:T(8,128)S(1)} fusion(s32[48]{0:T(128)S(1)} %copy-done.8, s32[12]{0:T(128)S(1)} %iota_add_fusion, bf16[6,8,32,2048]{3,2,1,0:T(8,128)(2,1)} %bitcast.79), kind=kOutput, calls=%fused_computation.1 | convolution fusion | flops 75498048 | bytes 9437424 | tf_op jit(solution)/shard_map/dot_general | solution.py:132
  609.1 3.5 copy.23
  612.6 17.1 %all-gather.6.cloned.1.call-done = bf16[48,32,1024]{2,1,0:T(8,128)(2,1)} async-done(((bf16[12,32,1024]{2,1,0:T(8,128)(2,1)}), bf16[48,32,1024]{2,1,0:T(8,128)(2,1)}) %all-gather.6.cloned.1.call-update) | async-done | bytes 3145744 | tf_op jit(solution)/shard_map/all_gather | solution.py:126
  629.7 5.3 fusion.9
  635.0 2.1 copy.24
  (12 shorter events, 0.1 us)
Async XLA Ops:
  7.2 365.9 %copy-start = (bf16[576,2048]{1,0:T(8,128)(2,1)S(1)}, bf16[576,2048]{1,0:T(8,128)(2,1)}, u32[]{:S(2)}) copy-start(bf16[576,2048]{1,0:T(8,128)(2,1)} %param.13) | copy-start | bytes 7077892
  7.2 6.0 copy-start.4
  7.2 13.3 %copy-start.7 = (s32[48]{0:T(128)S(1)}, s32[48]{0:T(128)}, u32[]{:S(2)}) copy-start(s32[48]{0:T(128)} %param.12) | copy-start | bytes 580
  7.2 32.1 %all-reduce.4.cloned.1.call-start = ((), (), s32[]{:S(2)}) async-start(), calls=%async_computation.4 | async-start | bytes 524288 | tf_op jit(solution)/shard_map/psum | solution.py:27
  13.2 271.2 %all-reduce.6.cloned.1.call-start = ((), (), s32[]{:S(2)}) async-start(), calls=%async_computation.5 | async-start | bytes 12582912 | tf_op jit(solution)/shard_map/psum | solution.py:35
  61.4 311.7 %all-reduce.8.cloned.1.call-start = ((), (), s32[]{:S(2)}) async-start(), calls=%async_computation.6 | async-start | bytes 6291456 | tf_op jit(solution)/shard_map/psum | solution.py:17
  288.1 107.5 %reduce-scatter.10.cloned.1.call-start = ((), (), s32[]{:S(2)}) async-start(), calls=%async_computation.10 | async-start | bytes 184320
  376.0 105.4 %reduce-scatter.6.cloned.1.call-start = ((), (), s32[]{:S(2)}) async-start(), calls=%async_computation.3 | async-start | bytes 5898240 | tf_op jit(solution)/shard_map/reduce_scatter | solution.py:65
  391.2 159.6 %reduce-scatter.8.cloned.1.call-start = ((), (), s32[]{:S(2)}) async-start(), calls=%async_computation.8 | async-start | bytes 3932160 | tf_op jit(solution)/shard_map/reduce_scatter | solution.py:89
  391.3 5.3 copy-start.5
  397.2 88.2 %copy-start.2 = (bf16[144,4096]{1,0:T(8,128)(2,1)S(1)}, bf16[144,4096]{1,0:T(8,128)(2,1)}, u32[]{:S(2)}) copy-start(bf16[144,4096]{1,0:T(8,128)(2,1)} %param.15) | copy-start | bytes 3538948
  481.4 4.1 copy-start.3
  485.5 2.7 copy-start.1
  488.2 0.7 copy-start.6
  488.2 111.4 %all-gather.4.cloned.1.call-start = ((), (), s32[]{:S(2)}) async-start(), calls=%async_computation.7 | async-start | bytes 7864320 | tf_op jit(solution)/shard_map/all_gather | solution.py:123
  533.7 65.9 %copy-start.8 = (s32[48]{0:T(128)S(1)}, s32[48]{0:T(128)}, u32[]{:S(2)}) copy-start(s32[48]{0:T(128)} %param.12) | copy-start | bytes 580
  535.4 94.2 %all-gather.6.cloned.1.call-start = ((), (), s32[]{:S(2)}) async-start(), calls=%async_computation.9 | async-start | bytes 3932160 | tf_op jit(solution)/shard_map/all_gather | solution.py:126
Sparse Core Ops, SparseCore 0:
  13.3 26.0 all-reduce.3
  61.5 222.8 all-reduce.5
  288.3 84.7 all-reduce.7
  376.1 19.5 reduce-scatter.9
  397.8 83.4 reduce-scatter.5
  488.3 62.4 reduce-scatter.7
  552.9 46.5 all-gather.3
  601.1 28.4 all-gather.5
where the time goes:
time: 644 us
  waiting for transfers between devices  482 us (75%)
  matrix products  73.3 us (11%)
  blocking collectives  56.7 us (9%)
  between operations  14.4 us (2%)
  local copies, waits for them, and re-layouts  8.55 us (1%)
  other arithmetic  7.99 us (1%)
    psum x1, waiting for transfers between devices, hypernet(): summed = lax.psum(partial_value.astype(jnp.bfloat16), 'tensor')  223 us
    psum x1, waiting for transfers between devices, spread(): return lax.psum(block, axis)  84.8 us
    reduce_scatter x1, waiting for transfers between devices, body(): lax.psum_scatter(base_part.astype(jnp.bfloat16), 'tensor', scatter_dimens...  84.1 us
    all_gather x1, waiting for transfers between devices, body(): lax.all_gather(lowering_matrix_sensitivity.astype(jnp.bfloat16), 'group',...  48.7 us
    psum x1, blocking collectives, body(): lax.psum(placed, ('tensor', 'dp')).astype(jnp.bfloat16)  40.6 us
    dot_general x1, matrix products, hypernet(): jnp.dot(hidden, hyper_out, preferred_element_type=jnp.float32)  18.5 us
    all_gather x1, waiting for transfers between devices, body(): lax.all_gather(grad_up_local.astype(jnp.bfloat16), 'group', axis=0, tiled...  17.1 us
    reduce_scatter x1, waiting for transfers between devices, body(): lax.psum_scatter(partial_up_gradient.reshape(doc_count, R, up_factor_rows...  15.1 us
  transfers between devices with their start and end apart: 8, of which 8 were waited for; matrix products, arithmetic and copies ran while one was open for 6% of the time, Pallas kernels for 0%

commit v1 on v0

--- a/solution.py
+++ b/solution.py
@@ -140,6 +140,200 @@
     return (adapted, grad_down, grad_up)
 
 
+def rotate(n, k):
+    return [(i, (i + k) % n) for i in range(n)]
+
+
+def flip(n, bit):
+    return [(i, i ^ bit) for i in range(n)]
+
+
+def pick(block, index, size=1):
+    return lax.dynamic_slice_in_dim(block, index, size, 0)
+
+
+def gather_flips(block, axis, size):
+    blocks = [block]
+    bits = []
+    bit = size // 2
+    order = [0]
+    stacked = block[None]
+    while bit:
+        stacked = jnp.concatenate([stacked, lax.ppermute(stacked, axis, flip(size, bit))], axis=0)
+        order = order + [k ^ bit for k in order]
+        bit //= 2
+    return stacked, order
+
+
+def line_sum(blocks, place):
+    lower = place < 2
+    sent = pick(blocks, jnp.where(place == 0, 1, 0), 3)
+    outer = lax.ppermute(sent, "tensor", [(0, 1), (3, 2)])
+    far = pick(blocks, jnp.where(lower, 2, 0), 2).astype(jnp.float32) + pick(
+        outer, jnp.where(lower, 1, 0), 2
+    ).astype(jnp.float32)
+    middle = lax.ppermute(far.astype(jnp.bfloat16), "tensor", [(1, 2), (2, 1)])
+    end = pick(blocks, jnp.where(lower, 0, 3)).astype(jnp.float32) + pick(
+        middle, jnp.where(lower, 0, 1)
+    ).astype(jnp.float32)
+    last = lax.ppermute(end.astype(jnp.bfloat16), "tensor", [(1, 0), (2, 3)])
+    return (
+        pick(blocks, place).astype(jnp.float32)
+        + pick(outer, jnp.where(lower, 0, 2)).astype(jnp.float32)
+        + pick(middle, jnp.where(lower, 1, 0)).astype(jnp.float32)
+        + last.astype(jnp.float32)
+    )[0]
+
+
+def line_gather(block, place):
+    right = [(0, 1), (1, 2), (2, 3)]
+    left = [(3, 2), (2, 1), (1, 0)]
+    r1 = lax.ppermute(block, "tensor", right)
+    l1 = lax.ppermute(block, "tensor", left)
+    r2 = lax.ppermute(r1, "tensor", right[1:])
+    l2 = lax.ppermute(l1, "tensor", left[1:])
+    x3 = lax.ppermute(jnp.where(place == 2, r2, l2), "tensor", [(2, 3), (1, 0)])
+    return jnp.stack(
+        [block, jnp.where(place == 0, x3, r1), jnp.where(place < 2, l2, r2), jnp.where(place == 3, x3, l1)]
+    )
+
+
+def aligned_body(doc_emb, row_emb, hyper_in, hyper_out, assign, states, proj_weight, targets):
+    groups = lax.axis_size("group")
+    line = lax.axis_size("tensor")
+    group, place, half = (lax.axis_index(a) for a in ("group", "tensor", "dp"))
+    docs = doc_emb.shape[0]
+    mine = docs // line
+    per_doc = states.shape[0] // docs
+    in_width = states.shape[1]
+    out_width = proj_weight.shape[1]
+    hidden_width = hyper_in.shape[1]
+    scale = 1.0 / math.sqrt(in_width * line)
+    f32, bf16 = jnp.float32, jnp.bfloat16
+
+    slot_docs = lax.dynamic_slice_in_dim(assign, group * docs, docs)
+    embs, order = gather_flips(doc_emb, "group", groups)
+    flips = jnp.array(order, jnp.int32)
+    there = (group ^ flips)[:, None] * docs + jnp.arange(docs, dtype=jnp.int32)[None, :]
+    chooser = (slot_docs[:, None] == there.reshape(1, -1)).astype(bf16)
+    chosen = jnp.dot(
+        chooser, embs.reshape(groups * docs, -1), preferred_element_type=f32
+    ).astype(bf16)
+
+    by_slot = states.reshape(line, mine, per_doc, in_width)
+    targets = targets.reshape(mine, per_doc, out_width)
+    base = []
+    for k in range(mine):
+        part = jnp.dot(
+            by_slot[:, k].reshape(line * per_doc, in_width), proj_weight, preferred_element_type=f32
+        ).astype(bf16)
+        base.append(line_sum(part.reshape(line, per_doc, out_width), place))
+
+    moved, _ = gather_flips(states, "group", groups)
+    own_docs = group * docs + jnp.arange(docs, dtype=jnp.int32)
+    owner = (own_docs[:, None] == assign[there.reshape(-1)][None, :]).astype(bf16)
+    own_states = jnp.dot(
+        owner, moved.reshape(groups * docs, per_doc * in_width), preferred_element_type=f32
+    ).astype(bf16).reshape(docs, per_doc, in_width)
+
+    pre = jnp.dot(
+        jnp.concatenate([row_emb, chosen], axis=0), hyper_in, preferred_element_type=f32
+    ).astype(bf16)
+    pre = pre.astype(f32) + lax.ppermute(pre, "dp", rotate(2, 1)).astype(f32)
+    pre_row, pre_doc = pre[: 2 * R], pre[2 * R :]
+
+    def hidden_of(doc_part, row_part):
+        return jax.nn.silu(doc_part[:, None, :] + row_part[None, :, :]).astype(bf16)
+
+    tokens_half = states.shape[0] // 2
+    piece = lax.dynamic_slice_in_dim(states, half * tokens_half, tokens_half, 0)
+    line_states = line_gather(piece, place)
+
+    def columns_of(which):
+        return jnp.concatenate(
+            [pick(line_states, (place - 2 * which - b) % line)[0] for b in range(2)], axis=1
+        )
+
+    kept = columns_of(half)
+    given = lax.ppermute(columns_of(1 - half), "dp", rotate(2, 1))
+    wide = jnp.concatenate([kept, given], axis=0)
+    through = lax.dot_general(
+        wide, hyper_out, (((1,), (1,)), ((), ())), preferred_element_type=f32
+    ).astype(bf16)
+    turned = jnp.where(half == 0, pre_doc, jnp.roll(pre_doc, docs // 2, axis=0))
+    hidden_down = hidden_of(turned, pre_row[:R])
+    low = jnp.einsum(
+        "quw,qlw->qul",
+        through.reshape(docs, per_doc, hidden_width),
+        hidden_down,
+        preferred_element_type=f32,
+    ).reshape(states.shape[0], R)
+    low = low + lax.ppermute(jnp.roll(low, tokens_half, axis=0), "dp", rotate(2, 1))
+    low = low.reshape(line, mine * per_doc, R)
+    low_mine = pick(low, (place - 2 * half) % line)
+    for k in range(1, line):
+        low_mine = low_mine + lax.ppermute(
+            pick(low, (place + k - 2 * half) % line), "tensor", rotate(line, k)
+        )
+    narrow = (low_mine[0] * scale).astype(bf16).reshape(mine, per_doc, R)
+
+    hidden_up = hidden_of(pre_doc, pre_row[R:]).reshape(line, mine, R, hidden_width)
+    adapted, up_out = [], []
+    quarter = out_width // line
+    for k in range(mine):
+        part = jnp.dot(
+            hidden_up[:, k].reshape(line * R, hidden_width), hyper_out, preferred_element_type=f32
+        ).astype(bf16)
+        up = line_sum(part.reshape(line, R, out_width), place).astype(bf16)
+        raised = base[k] + LOWDIM_MULTIPLE * jnp.dot(narrow[k], up, preferred_element_type=f32)
+        adapted.append(raised.astype(bf16))
+        residual = (raised - targets[k].astype(f32)).astype(bf16)
+        token = LOWDIM_MULTIPLE * lax.dot_general(
+            up, residual, (((1,), (1,)), ((), ())), preferred_element_type=f32
+        )
+        token = (token + lax.ppermute(token, "dp", rotate(2, 1))).astype(bf16)
+        token = jnp.pad(token, ((0, 0), (0, 128 - per_doc)))
+        up_grad = (
+            LOWDIM_MULTIPLE
+            * lax.dot_general(
+                narrow[k], residual, (((0,), (0,)), ((), ())), preferred_element_type=f32
+            )
+        ).astype(bf16)
+        got = []
+        for r in range(line):
+            block = jnp.concatenate(
+                [
+                    lax.dynamic_slice_in_dim(up_grad, (place + r) % line * quarter, quarter, 1),
+                    token,
+                ],
+                axis=1,
+            )
+            got.append(lax.ppermute(block, "tensor", rotate(line, r)) if r else block)
+        everyone, _ = gather_flips(jnp.stack(got), "group", groups)
+        up_out.append(everyone)
+
+    places = (place - jnp.arange(line, dtype=jnp.int32)) % line
+    slots = (
+        (group ^ flips)[None, :, None] * docs
+        + places[None, None, :] * mine
+        + jnp.arange(mine, dtype=jnp.int32)[:, None, None]
+    ).reshape(-1)
+    taker = (own_docs[:, None] == assign[slots][None, :]).astype(bf16)
+    gathered = jnp.stack(up_out).reshape(mine * groups * line, R, quarter + 128)
+    grad_up = jnp.dot(
+        taker,
+        gathered[:, :, :quarter].reshape(-1, R * quarter),
+        preferred_element_type=f32,
+    ).reshape(docs, R, quarter)
+    tokens = jnp.dot(
+        taker, gathered[:, :, quarter:].reshape(-1, R * 128), preferred_element_type=f32
+    ).astype(bf16).reshape(docs, R, 128)[:, :, :per_doc]
+    grad_down = scale * jnp.einsum(
+        "ode,oec->odc", tokens, own_states, preferred_element_type=f32
+    )
+    return (jnp.concatenate(adapted, axis=0), grad_down, grad_up)
+
+
 def solution(mesh):
     in_specs = (
         P("group", "dp"),
@@ -156,4 +350,12 @@
         P("group", None, "tensor"),
         P("group", None, ("dp", "tensor")),
     )
-    return jax.shard_map(body, mesh=mesh, in_specs=in_specs, out_specs=out_specs, check_vma=False)
+    groups, line, halves = (mesh.shape[a] for a in ("group", "tensor", "dp"))
+
+    def step(*arrays):
+        docs = arrays[0].shape[0] // groups
+        fits = line == 4 and halves == 2 and groups & (groups - 1) == 0 and docs % line == 0
+        plan = aligned_body if fits and docs % 2 == 0 else body
+        return jax.shard_map(plan, mesh=mesh, in_specs=in_specs, out_specs=out_specs, check_vma=False)(*arrays)
+
+    return step

time: 644 us -> 426 us (0.66)
  waiting for transfers between devices: 482 us -> 186 us
  starting transfers between devices: 0.73 us -> 78.3 us
  blocking collectives: 56.7 us -> 0 us
  local copies, waits for them, and re-layouts: 8.55 us -> 37.6 us
  other arithmetic: 7.99 us -> 27.7 us
  matrix products: 73.3 us -> 87.7 us
  between operations: 14.4 us -> 2.12 us
    psum x3 -> x0, waiting for transfers between devices: 313 us -> none  [the longest x1 223 us: hypernet(): summed = lax.psum(partial_value.astype(jnp.bfloat16), 'tensor')]
    ppermute x0 -> x51, waiting for transfers between devices: none -> 186 us  [the longest x1 78.2 us: line_gather(): x3 = lax.ppermute(jnp.where(place == 2, r2, l2), 'tensor', [(2, 3), (1, 0)])]
    reduce_scatter x2 -> x0, waiting for transfers between devices: 99.2 us -> none  [the longest x1 84.1 us: body(): lax.psum_scatter(base_part.astype(jnp.bfloat16), 'tensor', scatter_dimens...]
    ppermute x0 -> x51, starting transfers between devices: none -> 78.3 us  [the longest x9 18.9 us: aligned_body(): got.append(lax.ppermute(block, 'tensor', rotate(line, r)) if r else block)]
    all_gather x2 -> x0, waiting for transfers between devices: 65.8 us -> none  [the longest x1 48.7 us: body(): lax.all_gather(lowering_matrix_sensitivity.astype(jnp.bfloat16), 'group',...]
    psum x2 -> x0, blocking collectives: 49.5 us -> none  [the longest x1 40.6 us: body(): lax.psum(placed, ('tensor', 'dp')).astype(jnp.bfloat16)]
    dot_general x11 -> x23, matrix products: 73.3 us -> 87.7 us  [the longest x3 27.8 us: aligned_body(): jnp.dot(by_slot[:, k].reshape(line * per_doc, in_width), proj_weight, pre...]
    reshape x1 -> x5, local copies, waits for them, and re-layouts: 0.15 us -> 10.8 us  [the longest x1 10.5 us: aligned_body(): moved.reshape(groups * docs, per_doc * in_width)]
  transfers between devices with their start and end apart: 8 -> 51, of which waited for: 8 -> 16; matrix products, arithmetic and copies ran while one was open for 6% -> 29% of each run, Pallas kernels for 0% -> 0%
where the time goes in v1:
time: 426 us; the launch traced here: 420 us
  waiting for transfers between devices  186 us (44%)
  matrix products  87.7 us (21%)
  starting transfers between devices  78.3 us (18%)
  local copies, waits for them, and re-layouts  37.6 us (9%)
  other arithmetic  27.7 us (7%)
    ppermute x1, waiting for transfers between devices, line_gather(): x3 = lax.ppermute(jnp.where(place == 2, r2, l2), 'tensor', [(2, 3), (1, 0)])  78.2 us
    ppermute x6, waiting for transfers between devices, line_sum(): outer = lax.ppermute(sent, 'tensor', [(0, 1), (3, 2)])  47.4 us
    ppermute x1, waiting for transfers between devices, aligned_body(): given = lax.ppermute(columns_of(1 - half), 'dp', rotate(2, 1))  33.4 us
    dot_general x3, matrix products, aligned_body(): jnp.dot(by_slot[:, k].reshape(line * per_doc, in_width), proj_weight, pre...  27.8 us
    dot_general x3, matrix products, aligned_body(): jnp.dot(hidden_up[:, k].reshape(line * R, hidden_width), hyper_out, prefe...  19 us
    ppermute x9, starting transfers between devices, aligned_body(): got.append(lax.ppermute(block, 'tensor', rotate(line, r)) if r else block)  18.9 us
    ppermute x6, starting transfers between devices, line_sum(): outer = lax.ppermute(sent, 'tensor', [(0, 1), (3, 2)])  18 us
    dot_general x1, matrix products, aligned_body(): lax.dot_general(wide, hyper_out, (((1,), (1,)), ((), ())), preferred_elem...  15.5 us
  transfers between devices with their start and end apart: 51, of which 16 were waited for; matrix products, arithmetic and copies ran while one was open for 29% of the time, Pallas kernels for 0%

profile of v1, /device:TPU:0, one launch (start us, length us, event | category | flops | bytes accessed | tf_op | source)
XLA Modules:
  0.0 419.7 jit_solution(525938604748632792)
XLA Ops:
  0.6 2.6 constant_dynamic-slice_fusion.19
  3.2 6.0 %collective-permute-start.3 = (bf16[288,2048]{1,0:T(8,128)(2,1)}, bf16[288,2048]{1,0:T(8,128)(2,1)}, u32[]{:S(2)}, u32[]{:S(2)}) collective-permute-start(bf16[288,2048]{1,0:T(8,128)(2,1)} %constant_dynamic-slice_fusion.19), channel_id=1, source_target_pairs={{0,2},{2,4},{4,6},{1,3},{3,5},{5,7},{8,10},{10,12},{12,14},{9,11},... | collective-permute-start | bytes 3538952 | tf_op jit(solution)/shard_map/ppermute | solution.py:191
  10.5 1.6 collective-permute-start.9
  12.0 1.4 fusion.78
  13.4 9.4 %convolution_convert_fusion.1 = bf16[192,4096]{1,0:T(8,128)(2,1)S(1)} fusion(bf16[192,2048]{1,0:T(8,128)(2,1)} %bitcast.190, bf16[2048,4096]{1,0:T(8,128)(2,1)} %param.15), kind=kOutput, calls=%fused_computation.4 | convolution fusion | flops 3222011904 | bytes 19136512 | tf_op jit(solution)/shard_map/dot_general | solution.py:227
  24.0 5.7 %collective-permute-start.25 = (bf16[3,48,4096]{2,1,0:T(8,128)(2,1)}, bf16[3,48,4096]{2,1,0:T(8,128)(2,1)}, u32[]{:S(2)}, u32[]{:S(2)}) collective-permute-start(bf16[3,48,4096]{2,1,0:T(8,128)(2,1)} %constant_dynamic-slice_fusion.5), channel_id=1, source_target_pairs={{0,2},{6,4},{1,3},{7,5},{8,10},{14,12},{9,11},{15,13},{16,18},{22,... | collective-permute-start | bytes 3538952 | tf_op jit(solution)/shard_map/ppermute | solution.py:171
  29.7 9.2 %convolution_convert_fusion.3 = bf16[192,4096]{1,0:T(8,128)(2,1)S(1)} fusion(bf16[192,2048]{1,0:T(8,128)(2,1)S(1)} %bitcast.189, bf16[2048,4096]{1,0:T(8,128)(2,1)} %param.15), kind=kOutput, calls=%fused_computation.6 | convolution fusion | flops 3222011904 | bytes 19136512 | tf_op jit(solution)/shard_map/dot_general | solution.py:227
  41.2 2.8 collective-permute-start
  44.4 9.2 %convolution_convert_fusion.2 = bf16[192,4096]{1,0:T(8,128)(2,1)S(1)} fusion(bf16[192,2048]{1,0:T(8,128)(2,1)S(1)} %bitcast.188, bf16[2048,4096]{1,0:T(8,128)(2,1)} %param.15), kind=kOutput, calls=%fused_computation.5 | convolution fusion | flops 3222011904 | bytes 19136512 | tf_op jit(solution)/shard_map/dot_general | solution.py:227
  58.6 5.0 %convolution_convert_fusion.8 = bf16[76,2048]{1,0:T(8,128)(2,1)S(1)} fusion(bf16[2048,2048]{1,0:T(8,128)(2,1)} %param.11, bf16[12,2048]{1,0:T(8,128)(2,1)S(1)} %convolution_convert_fusion.9, bf16[64,2048]{1,0:T(8,128)(2,1)S(1)} %copy-done.25), kind=kOutput, calls=%fused_computation.48 | convolution fusion | flops 638312448 | bytes 9011200 | tf_op jit(solution)/shard_map/dot_general | solution.py:239
  63.5 1.6 collective-permute-start.11
  66.3 7.1 %collective-permute-done.11 = bf16[76,2048]{1,0:T(8,128)(2,1)S(1)} collective-permute-done((bf16[76,2048]{1,0:T(8,128)(2,1)S(1)}, bf16[76,2048]{1,0:T(8,128)(2,1)S(1)}, u32[]{:S(2)}, u32[]{:S(2)}) %collective-permute-start.11) | collective-permute-done | bytes 311328 | tf_op jit(solution)/shard_map/ppermute | solution.py:242
  73.4 2.5 collective-permute-start.19
  77.8 8.3 %convolution_convert_fusion.4 = bf16[128,4096]{1,0:T(8,128)(2,1)S(1)} fusion(bf16[128,2048]{1,0:T(8,128)(2,1)S(1)} %bitcast.186, bf16[2048,4096]{1,0:T(8,128)(2,1)} %param.12), kind=kOutput, calls=%fused_computation.7 | convolution fusion | flops 2148007936 | bytes 18350080 | tf_op jit(solution)/shard_map/dot_general | solution.py:284
  86.1 8.3 %convolution_convert_fusion.6 = bf16[128,4096]{1,0:T(8,128)(2,1)S(1)} fusion(bf16[128,2048]{1,0:T(8,128)(2,1)S(1)} %bitcast.185, bf16[2048,4096]{1,0:T(8,128)(2,1)} %param.12), kind=kOutput, calls=%fused_computation.9 | convolution fusion | flops 2148007936 | bytes 18350080 | tf_op jit(solution)/shard_map/dot_general | solution.py:284
  94.5 2.4 convolution_convert_fusion.5
  98.3 1.4 add_convert_fusion
  99.7 1.3 collective-permute-start.28
  102.4 8.3 %collective-permute-done.19 = bf16[3,48,4096]{2,1,0:T(8,128)(2,1)} collective-permute-done((bf16[3,48,4096]{2,1,0:T(8,128)(2,1)}, bf16[3,48,4096]{2,1,0:T(8,128)(2,1)}, u32[]{:S(2)}, u32[]{:S(2)}) %collective-permute-start.19) | collective-permute-done | bytes 1179680 | tf_op jit(solution)/shard_map/ppermute | solution.py:171
  110.7 4.4 %collective-permute-start.16 = (bf16[3,32,4096]{2,1,0:T(8,128)(2,1)S(1)}, bf16[3,32,4096]{2,1,0:T(8,128)(2,1)S(1)}, u32[]{:S(2)}, u32[]{:S(2)}) collective-permute-start(bf16[3,32,4096]{2,1,0:T(8,128)(2,1)S(1)} %constant_dynamic-slice_fusion.13), channel_id=1, source_target_pairs={{0,2},{6,4},{1,3},{7,5},{8,10},{14,12},{9,11},{15,13},{16,18},{22,... | collective-permute-start | bytes 2359304 | tf_op jit(solution)/shard_map/ppermute | solution.py:171
  118.6 8.9 %collective-permute-done.28 = bf16[3,32,4096]{2,1,0:T(8,128)(2,1)S(1)} collective-permute-done((bf16[3,32,4096]{2,1,0:T(8,128)(2,1)S(1)}, bf16[3,32,4096]{2,1,0:T(8,128)(2,1)S(1)}, u32[]{:S(2)}, u32[]{:S(2)}) %collective-permute-start.28) | collective-permute-done | bytes 786464 | tf_op jit(solution)/shard_map/ppermute | solution.py:171
  128.8 15.4 %collective-permute-done.16 = bf16[3,32,4096]{2,1,0:T(8,128)(2,1)S(1)} collective-permute-done((bf16[3,32,4096]{2,1,0:T(8,128)(2,1)S(1)}, bf16[3,32,4096]{2,1,0:T(8,128)(2,1)S(1)}, u32[]{:S(2)}, u32[]{:S(2)}) %collective-permute-start.16) | collective-permute-done | bytes 786464 | tf_op jit(solution)/shard_map/ppermute | solution.py:171
  145.1 14.9 %collective-permute-done.22 = bf16[3,32,4096]{2,1,0:T(8,128)(2,1)S(1)} collective-permute-done((bf16[3,32,4096]{2,1,0:T(8,128)(2,1)S(1)}, bf16[3,32,4096]{2,1,0:T(8,128)(2,1)S(1)}, u32[]{:S(2)}, u32[]{:S(2)}) %collective-permute-start.22) | collective-permute-done | bytes 786464 | tf_op jit(solution)/shard_map/ppermute | solution.py:171
  166.2 1.5 collective-permute-start.30
  168.5 78.2 %collective-permute-done.7 = bf16[288,2048]{1,0:T(8,128)(2,1)S(1)} collective-permute-done((bf16[288,2048]{1,0:T(8,128)(2,1)S(1)}, bf16[288,2048]{1,0:T(8,128)(2,1)S(1)}, u32[]{:S(2)}, u32[]{:S(2)}) %collective-permute-start.7) | collective-permute-done | bytes 1179680 | tf_op jit(solution)/shard_map/ppermute | solution.py:195
  248.0 1.5 select_bitcast_fusion.2
  250.1 1.5 dynamic-slice_bitcast_fusion.3
  252.0 1.6 collective-permute-start.8
  260.8 33.4 %collective-permute-done.8 = bf16[288,4096]{1,0:T(8,128)(2,1)S(1)} collective-permute-done((bf16[288,4096]{1,0:T(8,128)(2,1)S(1)}, bf16[288,4096]{1,0:T(8,128)(2,1)S(1)}, u32[]{:S(2)}, u32[]{:S(2)}) %collective-permute-start.8) | collective-permute-done | bytes 2359328 | tf_op jit(solution)/shard_map/ppermute | solution.py:258
  294.2 1.4 copy-done.26
  295.6 15.5 %fusion.20 = bf16[576,2048]{1,0:T(8,128)(2,1)} fusion(bf16[2048,4096]{1,0:T(8,128)(2,1)} %param.12, bf16[288,4096]{1,0:T(8,128)(2,1)} %copy-done.26, bf16[288,2048]{1,0:T(8,128)(2,1)} %get-tuple-element.15, bf16[288,2048]{1,0:T(8,128)(2,1)S(1)} %get-tuple-element.12), kind=kOutput, calls=%fused_computation.44 | convolution fusion | flops 9679011840 | bytes 23855104 | tf_op jit(solution)/shard_map/dot_general | solution.py:260
  311.1 2.6 fusion.24
  318.4 1.6 collective-permute-start.12
  320.0 1.9 fusion.35
  324.8 2.4 collective-permute-start.13
  327.2 1.4 collective-permute-start.14
  328.6 2.1 pad_maximum_fusion.2
  330.7 1.4 collective-permute-start.2
  332.3 1.8 fusion.84
  334.7 1.8 fusion.83
  337.0 3.5 collective-permute-done.2
  340.5 1.5 fusion.85
  342.5 1.5 collective-permute-start.43
  344.6 1.4 collective-permute-start.31
  346.1 2.2 collective-permute-done.31
  348.5 1.6 collective-permute-start.38
  350.1 2.8 collective-permute-start.39
  352.9 2.0 collective-permute-start.40
  355.9 2.4 collective-permute-done.39
  359.2 4.2 %collective-permute-start.46 = (bf16[32,1152]{1,0:T(8,128)(2,1)S(1)}, bf16[32,1152]{1,0:T(8,128)(2,1)S(1)}, u32[]{:S(2)}, u32[]{:S(2)}) collective-permute-start(bf16[32,1152]{1,0:T(8,128)(2,1)S(1)} %get-tuple-element.61), channel_id=1, source_target_pairs={{0,6},{2,0},{4,2},{6,4},{1,7},{3,1},{5,3},{7,5},{8,14},{10,8},{12,... | collective-permute-start | bytes 221192 | tf_op jit(solution)/shard_map/ppermute | solution.py:311
  363.5 2.1 collective-permute-start.33
  365.6 4.7 %collective-permute-start.34 = (bf16[32,1152]{1,0:T(8,128)(2,1)S(1)}, bf16[32,1152]{1,0:T(8,128)(2,1)S(1)}, u32[]{:S(2)}, u32[]{:S(2)}) collective-permute-start(bf16[32,1152]{1,0:T(8,128)(2,1)S(1)} %get-tuple-element.53), channel_id=1, source_target_pairs={{0,6},{2,0},{4,2},{6,4},{1,7},{3,1},{5,3},{7,5},{8,14},{10,8},{12,... | collective-permute-start | bytes 221192 | tf_op jit(solution)/shard_map/ppermute | solution.py:311
  370.3 1.5 collective-permute-start.41
  372.5 1.6 collective-permute-start.35
  374.0 4.4 %collective-permute-done.41 = bf16[1,4,32,1152]{3,2,1,0:T(8,128)(2,1)S(1)} collective-permute-done((bf16[1,4,32,1152]{3,2,1,0:T(8,128)(2,1)S(1)}, bf16[1,4,32,1152]{3,2,1,0:T(8,128)(2,1)S(1)}, u32[]{:S(2)}, u32[]{:S(2)}) %collective-permute-start.41) | collective-permute-done | bytes 294944 | tf_op jit(solution)/shard_map/ppermute | solution.py:162
  378.6 3.0 collective-permute-done.47
  381.8 3.0 collective-permute-done.35
  388.1 3.4 fusion.17
  391.6 2.1 copy.26
  393.9 6.0 %pad_maximum_fusion = bf16[4,576,2048]{2,1,0:T(8,128)(2,1)} fusion(bf16[2,576,2048]{2,1,0:T(8,128)(2,1)S(1)} %collective-permute-done.50, bf16[1,576,2048]{2,1,0:T(8,128)(2,1)} %collective-permute-done.49, bf16[1,576,2048]{2,1,0:T(8,128)(2,1)S(1)} %bitcast.154), kind=kLoop, calls=%fused_computation.3 | loop fusion | flops 9437184 | bytes 18874368 | tf_op jit(solution)/shard_map/concatenate | solution.py:162
  399.9 10.5 %reshape.238 = bf16[48,98304]{1,0:T(8,128)(2,1)} reshape(bf16[4,576,2048]{2,1,0:T(8,128)(2,1)} %pad_maximum_fusion) | data formatting | bytes 18874368 | tf_op jit(solution)/shard_map/reshape | solution.py:236
  410.4 5.1 %convolution_convert_fusion = bf16[12,98304]{1,0:T(8,128)(2,1)S(1)} fusion(bf16[48,98304]{1,0:T(8,128)(2,1)} %reshape.238, s32[48]{0:T(128)S(1)} %gather_fusion.1, s32[12]{0:T(128)S(1)} %iota_add_fusion.2), kind=kOutput, calls=%fused_computation.2 | convolution fusion | flops 114426432 | bytes 11796720 | tf_op jit(solution)/shard_map/dot_general | solution.py:235
  415.5 1.7 copy.34
  417.3 2.2 convolution_multiply_fusion.6
  (224 shorter events, 54.1 us)
Async XLA Ops:
  0.6 11.4 %copy-start.1 = (bf16[576,2048]{1,0:T(8,128)(2,1)S(1)}, bf16[576,2048]{1,0:T(8,128)(2,1)}, u32[]{:S(2)}) copy-start(bf16[576,2048]{1,0:T(8,128)(2,1)} %param.14) | copy-start | bytes 7077892
  3.2 113.2 %collective-permute-start.3 = (bf16[288,2048]{1,0:T(8,128)(2,1)}, bf16[288,2048]{1,0:T(8,128)(2,1)}, u32[]{:S(2)}, u32[]{:S(2)}) collective-permute-start(bf16[288,2048]{1,0:T(8,128)(2,1)} %constant_dynamic-slice_fusion.19), channel_id=1, source_target_pairs={{0,2},{2,4},{4,6},{1,3},{3,5},{5,7},{8,10},{10,12},{12,14},{9,11},... | collective-permute-start | bytes 3538952 | tf_op jit(solution)/shard_map/ppermute | solution.py:191
  9.2 108.6 %collective-permute-start.5 = (bf16[288,2048]{1,0:T(8,128)(2,1)}, bf16[288,2048]{1,0:T(8,128)(2,1)}, u32[]{:S(2)}, u32[]{:S(2)}) collective-permute-start(bf16[288,2048]{1,0:T(8,128)(2,1)} %constant_dynamic-slice_fusion.19), channel_id=1, source_target_pairs={{6,4},{4,2},{2,0},{7,5},{5,3},{3,1},{14,12},{12,10},{10,8},{15,13}... | collective-permute-start | bytes 3538952 | tf_op jit(solution)/shard_map/ppermute | solution.py:192
  10.5 46.3 %collective-permute-start.9 = (bf16[1,12,2048]{2,1,0:T(8,128)(2,1)}, bf16[1,12,2048]{2,1,0:T(8,128)(2,1)S(1)}, u32[]{:S(2)}, u32[]{:S(2)}) collective-permute-start(bf16[1,12,2048]{2,1,0:T(8,128)(2,1)} %bitcast.193), channel_id=1, source_target_pairs={{0,16},{8,24},{16,0},{24,8},{1,17},{9,25},{17,1},{25,9},{2,18},{10... | collective-permute-start | bytes 147464 | tf_op jit(solution)/shard_map/ppermute | solution.py:162
  24.0 73.1 %collective-permute-start.25 = (bf16[3,48,4096]{2,1,0:T(8,128)(2,1)}, bf16[3,48,4096]{2,1,0:T(8,128)(2,1)}, u32[]{:S(2)}, u32[]{:S(2)}) collective-permute-start(bf16[3,48,4096]{2,1,0:T(8,128)(2,1)} %constant_dynamic-slice_fusion.5), channel_id=1, source_target_pairs={{0,2},{6,4},{1,3},{7,5},{8,10},{14,12},{9,11},{15,13},{16,18},{22,... | collective-permute-start | bytes 3538952 | tf_op jit(solution)/shard_map/ppermute | solution.py:171
  41.2 58.4 %collective-permute-start = (bf16[3,48,4096]{2,1,0:T(8,128)(2,1)}, bf16[3,48,4096]{2,1,0:T(8,128)(2,1)}, u32[]{:S(2)}, u32[]{:S(2)}) collective-permute-start(bf16[3,48,4096]{2,1,0:T(8,128)(2,1)} %constant_dynamic-slice_fusion.22), channel_id=1, source_target_pairs={{0,2},{6,4},{1,3},{7,5},{8,10},{14,12},{9,11},{15,13},{16,18},{22,... | collective-permute-start | bytes 3538952 | tf_op jit(solution)/shard_map/ppermute | solution.py:171
  56.9 1.4 collective-permute-start.10
  63.5 9.8 %collective-permute-start.11 = (bf16[76,2048]{1,0:T(8,128)(2,1)S(1)}, bf16[76,2048]{1,0:T(8,128)(2,1)S(1)}, u32[]{:S(2)}, u32[]{:S(2)}) collective-permute-start(bf16[76,2048]{1,0:T(8,128)(2,1)S(1)} %convolution_convert_fusion.8), channel_id=1, source_target_pairs={{0,1},{1,0},{2,3},{3,2},{4,5},{5,4},{6,7},{7,6},{8,9},{9,8},{10,11... | collective-permute-start | bytes 933896 | tf_op jit(solution)/shard_map/ppermute | solution.py:242
  73.4 37.3 %collective-permute-start.19 = (bf16[3,48,4096]{2,1,0:T(8,128)(2,1)}, bf16[3,48,4096]{2,1,0:T(8,128)(2,1)}, u32[]{:S(2)}, u32[]{:S(2)}) collective-permute-start(bf16[3,48,4096]{2,1,0:T(8,128)(2,1)} %constant_dynamic-slice_fusion.11), channel_id=1, source_target_pairs={{0,2},{6,4},{1,3},{7,5},{8,10},{14,12},{9,11},{15,13},{16,18},{22,... | collective-permute-start | bytes 3538952 | tf_op jit(solution)/shard_map/ppermute | solution.py:171
  77.8 16.7 %slice-start = ((s8[16777216]{0:T(1024)(128)(4,1)}), s8[4194304]{0:T(1024)(128)(4,1)S(1)}, s32[]{:S(2)}) async-start(s8[16777216]{0:T(1024)(128)(4,1)} %bitcast.149), calls=%async_computation | async-start | bytes 8388608
  77.8 16.6 %slice-start.1 = ((s8[16777216]{0:T(1024)(128)(4,1)}), s8[4194304]{0:T(1024)(128)(4,1)S(1)}, s32[]{:S(2)}) async-start(s8[16777216]{0:T(1024)(128)(4,1)} %bitcast.149), calls=%async_computation.1 | async-start | bytes 8388608
  86.1 8.3 %slice-start.2 = ((s8[16777216]{0:T(1024)(128)(4,1)}), s8[4194304]{0:T(1024)(128)(4,1)S(1)}, s32[]{:S(2)}) async-start(s8[16777216]{0:T(1024)(128)(4,1)} %bitcast.149), calls=%async_computation.2 | async-start | bytes 8388608
  86.1 8.3 %slice-start.3 = ((s8[16777216]{0:T(1024)(128)(4,1)}), s8[4194304]{0:T(1024)(128)(4,1)S(1)}, s32[]{:S(2)}) async-start(s8[16777216]{0:T(1024)(128)(4,1)} %bitcast.149), calls=%async_computation.3 | async-start | bytes 8388608
  97.1 18.0 %copy-start.7 = (bf16[192,4096]{1,0:T(8,128)(2,1)S(1)}, bf16[192,4096]{1,0:T(8,128)(2,1)}, u32[]{:S(2)}) copy-start(bf16[192,4096]{1,0:T(8,128)(2,1)} %copy-done.6) | copy-start | bytes 4718596
  97.1 230.0 %collective-permute-start.49 = (bf16[1,576,2048]{2,1,0:T(8,128)(2,1)S(1)}, bf16[1,576,2048]{2,1,0:T(8,128)(2,1)}, u32[]{:S(2)}, u32[]{:S(2)}) collective-permute-start(bf16[1,576,2048]{2,1,0:T(8,128)(2,1)S(1)} %bitcast.152), channel_id=1, source_target_pairs={{0,16},{8,24},{16,0},{24,8},{1,17},{9,25},{17,1},{25,9},{2,18},{10... | collective-permute-start | bytes 7077896 | tf_op jit(solution)/shard_map/ppermute | solution.py:162
  99.7 27.7 %collective-permute-start.28 = (bf16[3,32,4096]{2,1,0:T(8,128)(2,1)S(1)}, bf16[3,32,4096]{2,1,0:T(8,128)(2,1)S(1)}, u32[]{:S(2)}, u32[]{:S(2)}) collective-permute-start(bf16[3,32,4096]{2,1,0:T(8,128)(2,1)S(1)} %constant_dynamic-slice_fusion.1), channel_id=1, source_target_pairs={{0,2},{6,4},{1,3},{7,5},{8,10},{14,12},{9,11},{15,13},{16,18},{22,... | collective-permute-start | bytes 2359304 | tf_op jit(solution)/shard_map/ppermute | solution.py:171
  110.7 33.6 %collective-permute-start.16 = (bf16[3,32,4096]{2,1,0:T(8,128)(2,1)S(1)}, bf16[3,32,4096]{2,1,0:T(8,128)(2,1)S(1)}, u32[]{:S(2)}, u32[]{:S(2)}) collective-permute-start(bf16[3,32,4096]{2,1,0:T(8,128)(2,1)S(1)} %constant_dynamic-slice_fusion.13), channel_id=1, source_target_pairs={{0,2},{6,4},{1,3},{7,5},{8,10},{14,12},{9,11},{15,13},{16,18},{22,... | collective-permute-start | bytes 2359304 | tf_op jit(solution)/shard_map/ppermute | solution.py:171
  116.4 43.5 %collective-permute-start.22 = (bf16[3,32,4096]{2,1,0:T(8,128)(2,1)S(1)}, bf16[3,32,4096]{2,1,0:T(8,128)(2,1)S(1)}, u32[]{:S(2)}, u32[]{:S(2)}) collective-permute-start(bf16[3,32,4096]{2,1,0:T(8,128)(2,1)S(1)} %constant_dynamic-slice_fusion.9), channel_id=1, source_target_pairs={{0,2},{6,4},{1,3},{7,5},{8,10},{14,12},{9,11},{15,13},{16,18},{22,... | collective-permute-start | bytes 2359304 | tf_op jit(solution)/shard_map/ppermute | solution.py:171
  117.8 43.8 %collective-permute-start.4 = (bf16[288,2048]{1,0:T(8,128)(2,1)}, bf16[288,2048]{1,0:T(8,128)(2,1)S(1)}, u32[]{:S(2)}, u32[]{:S(2)}) collective-permute-start(bf16[288,2048]{1,0:T(8,128)(2,1)} %collective-permute-done.3), channel_id=1, source_target_pairs={{2,4},{4,6},{3,5},{5,7},{10,12},{12,14},{11,13},{13,15},{18,20},{2... | collective-permute-start | bytes 3538952 | tf_op jit(solution)/shard_map/ppermute | solution.py:193
  127.4 34.9 %collective-permute-start.6 = (bf16[288,2048]{1,0:T(8,128)(2,1)}, bf16[288,2048]{1,0:T(8,128)(2,1)S(1)}, u32[]{:S(2)}, u32[]{:S(2)}) collective-permute-start(bf16[288,2048]{1,0:T(8,128)(2,1)} %collective-permute-done.5), channel_id=1, source_target_pairs={{4,2},{2,0},{5,3},{3,1},{12,10},{10,8},{13,11},{11,9},{20,18},{18,... | collective-permute-start | bytes 3538952 | tf_op jit(solution)/shard_map/ppermute | solution.py:194
  144.3 16.6 %collective-permute-start.29 = (bf16[2,32,4096]{2,1,0:T(8,128)(2,1)S(1)}, bf16[2,32,4096]{2,1,0:T(8,128)(2,1)S(1)}, u32[]{:S(2)}, u32[]{:S(2)}) collective-permute-start(bf16[2,32,4096]{2,1,0:T(8,128)(2,1)S(1)} %add_convert_fusion.3), channel_id=1, source_target_pairs={{2,4},{4,2},{3,5},{5,3},{10,12},{12,10},{11,13},{13,11},{18,20},{2... | collective-permute-start | bytes 1572872 | tf_op jit(solution)/shard_map/ppermute | solution.py:175
  160.0 6.2 %collective-permute-start.26 = (bf16[2,48,4096]{2,1,0:T(8,128)(2,1)S(1)}, bf16[2,48,4096]{2,1,0:T(8,128)(2,1)S(1)}, u32[]{:S(2)}, u32[]{:S(2)}) collective-permute-start(bf16[2,48,4096]{2,1,0:T(8,128)(2,1)S(1)} %add_convert_fusion), channel_id=1, source_target_pairs={{2,4},{4,2},{3,5},{5,3},{10,12},{12,10},{11,13},{13,11},{18,20},{2... | collective-permute-start | bytes 2359304 | tf_op jit(solution)/shard_map/ppermute | solution.py:175
  160.8 91.1 %collective-permute-start.1 = (bf16[2,48,4096]{2,1,0:T(8,128)(2,1)S(1)}, bf16[2,48,4096]{2,1,0:T(8,128)(2,1)S(1)}, u32[]{:S(2)}, u32[]{:S(2)}) collective-permute-start(bf16[2,48,4096]{2,1,0:T(8,128)(2,1)S(1)} %add_convert_fusion.2), channel_id=1, source_target_pairs={{2,4},{4,2},{3,5},{5,3},{10,12},{12,10},{11,13},{13,11},{18,20},{2... | collective-permute-start | bytes 2359304 | tf_op jit(solution)/shard_map/ppermute | solution.py:175
  161.6 1.6 collective-permute-start.17
  162.4 2.3 collective-permute-start.23
  163.2 83.5 %collective-permute-start.7 = (bf16[288,2048]{1,0:T(8,128)(2,1)S(1)}, bf16[288,2048]{1,0:T(8,128)(2,1)S(1)}, u32[]{:S(2)}, u32[]{:S(2)}) collective-permute-start(bf16[288,2048]{1,0:T(8,128)(2,1)S(1)} %get-tuple-element.20), channel_id=1, source_target_pairs={{4,6},{2,0},{5,7},{3,1},{12,14},{10,8},{13,15},{11,9},{20,22},{18,... | collective-permute-start | bytes 3538952 | tf_op jit(solution)/shard_map/ppermute | solution.py:195
  164.6 84.8 %copy-start.22 = (bf16[2,32,4096]{2,1,0:T(8,128)(2,1)}, bf16[2,32,4096]{2,1,0:T(8,128)(2,1)S(1)}, u32[]{:S(2)}) copy-start(bf16[2,32,4096]{2,1,0:T(8,128)(2,1)S(1)} %collective-permute-done.23) | copy-start | bytes 1572868
  164.7 89.7 %collective-permute-start.20 = (bf16[2,48,4096]{2,1,0:T(8,128)(2,1)S(1)}, bf16[2,48,4096]{2,1,0:T(8,128)(2,1)S(1)}, u32[]{:S(2)}, u32[]{:S(2)}) collective-permute-start(bf16[2,48,4096]{2,1,0:T(8,128)(2,1)S(1)} %add_convert_fusion.1), channel_id=1, source_target_pairs={{2,4},{4,2},{3,5},{5,3},{10,12},{12,10},{11,13},{13,11},{18,20},{2... | collective-permute-start | bytes 2359304 | tf_op jit(solution)/shard_map/ppermute | solution.py:175
  166.2 80.6 %copy-start.17 = (bf16[2,48,4096]{2,1,0:T(8,128)(2,1)}, bf16[2,48,4096]{2,1,0:T(8,128)(2,1)S(1)}, u32[]{:S(2)}) copy-start(bf16[2,48,4096]{2,1,0:T(8,128)(2,1)S(1)} %collective-permute-done.26) | copy-start | bytes 2359300
  166.2 90.4 %collective-permute-start.30 = (bf16[1,32,4096]{2,1,0:T(8,128)(2,1)S(1)}, bf16[1,32,4096]{2,1,0:T(8,128)(2,1)S(1)}, u32[]{:S(2)}, u32[]{:S(2)}) collective-permute-start(bf16[1,32,4096]{2,1,0:T(8,128)(2,1)S(1)} %add_convert_fusion.10), channel_id=1, source_target_pairs={{2,0},{4,6},{3,1},{5,7},{10,8},{12,14},{11,9},{13,15},{18,16},{20,... | collective-permute-start | bytes 786440 | tf_op jit(solution)/shard_map/ppermute | solution.py:179
  168.5 81.0 %copy-start.8 = (bf16[1,288,2048]{2,1,0:T(8,128)(2,1)S(1)}, bf16[1,288,2048]{2,1,0:T(8,128)(2,1)}, u32[]{:S(2)}) copy-start(bf16[1,288,2048]{2,1,0:T(8,128)(2,1)} %fusion.109) | copy-start | bytes 3538948
  246.7 12.0 %collective-permute-start.18 = (bf16[1,32,4096]{2,1,0:T(8,128)(2,1)S(1)}, bf16[1,32,4096]{2,1,0:T(8,128)(2,1)S(1)}, u32[]{:S(2)}, u32[]{:S(2)}) collective-permute-start(bf16[1,32,4096]{2,1,0:T(8,128)(2,1)S(1)} %add_convert_fusion.14), channel_id=1, source_target_pairs={{2,0},{4,6},{3,1},{5,7},{10,8},{12,14},{11,9},{13,15},{18,16},{20,... | collective-permute-start | bytes 786440 | tf_op jit(solution)/shard_map/ppermute | solution.py:179
  251.9 8.9 %copy-start.15 = (bf16[2,48,4096]{2,1,0:T(8,128)(2,1)}, bf16[2,48,4096]{2,1,0:T(8,128)(2,1)S(1)}, u32[]{:S(2)}) copy-start(bf16[2,48,4096]{2,1,0:T(8,128)(2,1)S(1)} %collective-permute-done.1) | copy-start | bytes 2359300
  252.0 42.2 %collective-permute-start.8 = (bf16[288,4096]{1,0:T(8,128)(2,1)S(1)}, bf16[288,4096]{1,0:T(8,128)(2,1)S(1)}, u32[]{:S(2)}, u32[]{:S(2)}) collective-permute-start(bf16[288,4096]{1,0:T(8,128)(2,1)S(1)} %pad_maximum_fusion.4), channel_id=1, source_target_pairs={{0,1},{1,0},{2,3},{3,2},{4,5},{5,4},{6,7},{7,6},{8,9},{9,8},{10,11... | collective-permute-start | bytes 7077896 | tf_op jit(solution)/shard_map/ppermute | solution.py:258
  254.4 39.8 %copy-start.19 = (bf16[2,48,4096]{2,1,0:T(8,128)(2,1)}, bf16[2,48,4096]{2,1,0:T(8,128)(2,1)S(1)}, u32[]{:S(2)}) copy-start(bf16[2,48,4096]{2,1,0:T(8,128)(2,1)S(1)} %collective-permute-done.20) | copy-start | bytes 2359300
  254.4 65.6 %collective-permute-start.24 = (bf16[1,32,4096]{2,1,0:T(8,128)(2,1)}, bf16[1,32,4096]{2,1,0:T(8,128)(2,1)}, u32[]{:S(2)}, u32[]{:S(2)}) collective-permute-start(bf16[1,32,4096]{2,1,0:T(8,128)(2,1)} %add_convert_fusion.12), channel_id=1, source_target_pairs={{2,0},{4,6},{3,1},{5,7},{10,8},{12,14},{11,9},{13,15},{18,16},{20,... | collective-permute-start | bytes 786440 | tf_op jit(solution)/shard_map/ppermute | solution.py:179
  256.5 78.1 %collective-permute-start.27 = (bf16[1,48,4096]{2,1,0:T(8,128)(2,1)}, bf16[1,48,4096]{2,1,0:T(8,128)(2,1)}, u32[]{:S(2)}, u32[]{:S(2)}) collective-permute-start(bf16[1,48,4096]{2,1,0:T(8,128)(2,1)} %add_convert_fusion.6), channel_id=1, source_target_pairs={{2,0},{4,6},{3,1},{5,7},{10,8},{12,14},{11,9},{13,15},{18,16},{20,... | collective-permute-start | bytes 1179656 | tf_op jit(solution)/shard_map/ppermute | solution.py:179
  258.7 73.6 %collective-permute-start.21 = (bf16[1,48,4096]{2,1,0:T(8,128)(2,1)}, bf16[1,48,4096]{2,1,0:T(8,128)(2,1)}, u32[]{:S(2)}, u32[]{:S(2)}) collective-permute-start(bf16[1,48,4096]{2,1,0:T(8,128)(2,1)} %add_convert_fusion.7), channel_id=1, source_target_pairs={{2,0},{4,6},{3,1},{5,7},{10,8},{12,14},{11,9},{13,15},{18,16},{20,... | collective-permute-start | bytes 1179656 | tf_op jit(solution)/shard_map/ppermute | solution.py:179
  318.4 4.7 %collective-permute-start.12 = (f32[576,32]{0,1:T(8,128)S(1)}, f32[576,32]{0,1:T(8,128)}, u32[]{:S(2)}, u32[]{:S(2)}) collective-permute-start(f32[576,32]{0,1:T(8,128)S(1)} %pad_maximum_fusion.11), channel_id=1, source_target_pairs={{0,1},{1,0},{2,3},{3,2},{4,5},{5,4},{6,7},{7,6},{8,9},{9,8},{10,11... | collective-permute-start | bytes 221192 | tf_op jit(solution)/shard_map/ppermute | solution.py:271
  324.3 8.0 %copy-start.12 = (bf16[32,4096]{1,0:T(8,128)(2,1)S(1)}, bf16[32,4096]{1,0:T(8,128)(2,1)}, u32[]{:S(2)}) copy-start(bf16[32,4096]{1,0:T(8,128)(2,1)} %fusion.35) | copy-start | bytes 786436
  324.3 8.0 %copy-start.20 = (bf16[2,48,4096]{2,1,0:T(8,128)(2,1)S(1)}, bf16[2,48,4096]{2,1,0:T(8,128)(2,1)}, u32[]{:S(2)}) copy-start(bf16[2,48,4096]{2,1,0:T(8,128)(2,1)} %copy-done.19) | copy-start | bytes 2359300
  324.3 6.4 %collective-permute-start.15 = (f32[1,144,32]{1,2,0:T(8,128)S(1)}, f32[1,144,32]{1,2,0:T(8,128)S(1)}, u32[]{:S(2)}, u32[]{:S(2)}) collective-permute-start(f32[1,144,32]{1,2,0:T(8,128)S(1)} %copy.30), channel_id=1, source_target_pairs={{0,6},{2,0},{4,2},{6,4},{1,7},{3,1},{5,3},{7,5},{8,14},{10,8},{12,... | collective-permute-start | bytes 55304 | tf_op jit(solution)/shard_map/ppermute | solution.py:275
  324.8 7.3 %collective-permute-start.13 = (f32[1,144,32]{1,2,0:T(8,128)S(1)}, f32[1,144,32]{1,2,0:T(8,128)S(1)}, u32[]{:S(2)}, u32[]{:S(2)}) collective-permute-start(f32[1,144,32]{1,2,0:T(8,128)S(1)} %copy.28), channel_id=1, source_target_pairs={{0,2},{2,4},{4,6},{6,0},{1,3},{3,5},{5,7},{7,1},{8,10},{10,12},{12... | collective-permute-start | bytes 55304 | tf_op jit(solution)/shard_map/ppermute | solution.py:275
  327.2 5.1 %collective-permute-start.14 = (f32[1,144,32]{1,2,0:T(8,128)S(1)}, f32[1,144,32]{1,2,0:T(8,128)S(1)}, u32[]{:S(2)}, u32[]{:S(2)}) collective-permute-start(f32[1,144,32]{1,2,0:T(8,128)S(1)} %copy.29), channel_id=1, source_target_pairs={{0,4},{2,6},{4,0},{6,2},{1,5},{3,7},{5,1},{7,3},{8,12},{10,14},{12... | collective-permute-start | bytes 55304 | tf_op jit(solution)/shard_map/ppermute | solution.py:275
  330.7 9.8 %collective-permute-start.2 = (bf16[1,48,4096]{2,1,0:T(8,128)(2,1)S(1)}, bf16[1,48,4096]{2,1,0:T(8,128)(2,1)S(1)}, u32[]{:S(2)}, u32[]{:S(2)}) collective-permute-start(bf16[1,48,4096]{2,1,0:T(8,128)(2,1)S(1)} %copy-done.23), channel_id=1, source_target_pairs={{2,0},{4,6},{3,1},{5,7},{10,8},{12,14},{11,9},{13,15},{18,16},{20,... | collective-permute-start | bytes 1179656 | tf_op jit(solution)/shard_map/ppermute | solution.py:179
  332.2 61.8 %collective-permute-start.50 = (bf16[2,576,2048]{2,1,0:T(8,128)(2,1)S(1)}, bf16[2,576,2048]{2,1,0:T(8,128)(2,1)S(1)}, u32[]{:S(2)}, u32[]{:S(2)}) collective-permute-start(bf16[2,576,2048]{2,1,0:T(8,128)(2,1)S(1)} %pad_maximum_fusion.2), channel_id=1, source_target_pairs={{0,8},{8,0},{16,24},{24,16},{1,9},{9,1},{17,25},{25,17},{2,10},{10... | collective-permute-start | bytes 14155784 | tf_op jit(solution)/shard_map/ppermute | solution.py:162
  342.5 10.4 %collective-permute-start.43 = (f32[32,48]{1,0:T(8,128)S(1)}, f32[32,48]{1,0:T(8,128)S(1)}, u32[]{:S(2)}, u32[]{:S(2)}) collective-permute-start(f32[32,48]{1,0:T(8,128)S(1)} %convolution_multiply_fusion.7), channel_id=1, source_target_pairs={{0,1},{1,0},{2,3},{3,2},{4,5},{5,4},{6,7},{7,6},{8,9},{9,8},{10,11... | collective-permute-start | bytes 18440 | tf_op jit(solution)/shard_map/ppermute | solution.py:294
  344.0 4.5 %collective-permute-start.37 = (f32[32,48]{1,0:T(8,128)S(1)}, f32[32,48]{1,0:T(8,128)S(1)}, u32[]{:S(2)}, u32[]{:S(2)}) collective-permute-start(f32[32,48]{1,0:T(8,128)S(1)} %convolution_multiply_fusion.8), channel_id=1, source_target_pairs={{0,1},{1,0},{2,3},{3,2},{4,5},{5,4},{6,7},{7,6},{8,9},{9,8},{10,11... | collective-permute-start | bytes 18440 | tf_op jit(solution)/shard_map/ppermute | solution.py:294
  344.6 3.7 collective-permute-start.31
  348.4 23.4 %collective-permute-start.32 = (bf16[32,1152]{1,0:T(8,128)(2,1)S(1)}, bf16[32,1152]{1,0:T(8,128)(2,1)S(1)}, u32[]{:S(2)}, u32[]{:S(2)}) collective-permute-start(bf16[32,1152]{1,0:T(8,128)(2,1)S(1)} %get-tuple-element.51), channel_id=1, source_target_pairs={{0,2},{2,4},{4,6},{6,0},{1,3},{3,5},{5,7},{7,1},{8,10},{10,12},{12... | collective-permute-start | bytes 221192 | tf_op jit(solution)/shard_map/ppermute | solution.py:311
  348.5 7.0 %collective-permute-start.38 = (bf16[32,1152]{1,0:T(8,128)(2,1)S(1)}, bf16[32,1152]{1,0:T(8,128)(2,1)S(1)}, u32[]{:S(2)}, u32[]{:S(2)}) collective-permute-start(bf16[32,1152]{1,0:T(8,128)(2,1)S(1)} %get-tuple-element.55), channel_id=1, source_target_pairs={{0,2},{2,4},{4,6},{6,0},{1,3},{3,5},{5,7},{7,1},{8,10},{10,12},{12... | collective-permute-start | bytes 221192 | tf_op jit(solution)/shard_map/ppermute | solution.py:311
  350.1 8.2 %collective-permute-start.39 = (bf16[32,1152]{1,0:T(8,128)(2,1)S(1)}, bf16[32,1152]{1,0:T(8,128)(2,1)S(1)}, u32[]{:S(2)}, u32[]{:S(2)}) collective-permute-start(bf16[32,1152]{1,0:T(8,128)(2,1)S(1)} %get-tuple-element.56), channel_id=1, source_target_pairs={{0,4},{2,6},{4,0},{6,2},{1,5},{3,7},{5,1},{7,3},{8,12},{10,14},{12... | collective-permute-start | bytes 221192 | tf_op jit(solution)/shard_map/ppermute | solution.py:311
  352.9 6.3 %collective-permute-start.40 = (bf16[32,1152]{1,0:T(8,128)(2,1)S(1)}, bf16[32,1152]{1,0:T(8,128)(2,1)S(1)}, u32[]{:S(2)}, u32[]{:S(2)}) collective-permute-start(bf16[32,1152]{1,0:T(8,128)(2,1)S(1)} %get-tuple-element.57), channel_id=1, source_target_pairs={{0,6},{2,0},{4,2},{6,4},{1,7},{3,1},{5,3},{7,5},{8,14},{10,8},{12,... | collective-permute-start | bytes 221192 | tf_op jit(solution)/shard_map/ppermute | solution.py:311
  355.5 8.1 %collective-permute-start.44 = (bf16[32,1152]{1,0:T(8,128)(2,1)S(1)}, bf16[32,1152]{1,0:T(8,128)(2,1)S(1)}, u32[]{:S(2)}, u32[]{:S(2)}) collective-permute-start(bf16[32,1152]{1,0:T(8,128)(2,1)S(1)} %get-tuple-element.59), channel_id=1, source_target_pairs={{0,2},{2,4},{4,6},{6,0},{1,3},{3,5},{5,7},{7,1},{8,10},{10,12},{12... | collective-permute-start | bytes 221192 | tf_op jit(solution)/shard_map/ppermute | solution.py:311
  358.3 7.4 %collective-permute-start.45 = (bf16[32,1152]{1,0:T(8,128)(2,1)S(1)}, bf16[32,1152]{1,0:T(8,128)(2,1)S(1)}, u32[]{:S(2)}, u32[]{:S(2)}) collective-permute-start(bf16[32,1152]{1,0:T(8,128)(2,1)S(1)} %get-tuple-element.60), channel_id=1, source_target_pairs={{0,4},{2,6},{4,0},{6,2},{1,5},{3,7},{5,1},{7,3},{8,12},{10,14},{12... | collective-permute-start | bytes 221192 | tf_op jit(solution)/shard_map/ppermute | solution.py:311
  359.2 11.1 %collective-permute-start.46 = (bf16[32,1152]{1,0:T(8,128)(2,1)S(1)}, bf16[32,1152]{1,0:T(8,128)(2,1)S(1)}, u32[]{:S(2)}, u32[]{:S(2)}) collective-permute-start(bf16[32,1152]{1,0:T(8,128)(2,1)S(1)} %get-tuple-element.61), channel_id=1, source_target_pairs={{0,6},{2,0},{4,2},{6,4},{1,7},{3,1},{5,3},{7,5},{8,14},{10,8},{12,... | collective-permute-start | bytes 221192 | tf_op jit(solution)/shard_map/ppermute | solution.py:311
  363.5 8.9 %collective-permute-start.33 = (bf16[32,1152]{1,0:T(8,128)(2,1)S(1)}, bf16[32,1152]{1,0:T(8,128)(2,1)S(1)}, u32[]{:S(2)}, u32[]{:S(2)}) collective-permute-start(bf16[32,1152]{1,0:T(8,128)(2,1)S(1)} %get-tuple-element.52), channel_id=1, source_target_pairs={{0,4},{2,6},{4,0},{6,2},{1,5},{3,7},{5,1},{7,3},{8,12},{10,14},{12... | collective-permute-start | bytes 221192 | tf_op jit(solution)/shard_map/ppermute | solution.py:311
  365.6 6.8 %collective-permute-start.34 = (bf16[32,1152]{1,0:T(8,128)(2,1)S(1)}, bf16[32,1152]{1,0:T(8,128)(2,1)S(1)}, u32[]{:S(2)}, u32[]{:S(2)}) collective-permute-start(bf16[32,1152]{1,0:T(8,128)(2,1)S(1)} %get-tuple-element.53), channel_id=1, source_target_pairs={{0,6},{2,0},{4,2},{6,4},{1,7},{3,1},{5,3},{7,5},{8,14},{10,8},{12,... | collective-permute-start | bytes 221192 | tf_op jit(solution)/shard_map/ppermute | solution.py:311
  370.3 8.2 %collective-permute-start.41 = (bf16[1,4,32,1152]{3,2,1,0:T(8,128)(2,1)S(1)}, bf16[1,4,32,1152]{3,2,1,0:T(8,128)(2,1)S(1)}, u32[]{:S(2)}, u32[]{:S(2)}) collective-permute-start(bf16[1,4,32,1152]{3,2,1,0:T(8,128)(2,1)S(1)} %maximum_bitcast_fusion.4), channel_id=1, source_target_pairs={{0,16},{8,24},{16,0},{24,8},{1,17},{9,25},{17,1},{25,9},{2,18},{10... | collective-permute-start | bytes 884744 | tf_op jit(solution)/shard_map/ppermute | solution.py:162
  371.8 9.8 %collective-permute-start.47 = (bf16[1,4,32,1152]{3,2,1,0:T(8,128)(2,1)S(1)}, bf16[1,4,32,1152]{3,2,1,0:T(8,128)(2,1)S(1)}, u32[]{:S(2)}, u32[]{:S(2)}) collective-permute-start(bf16[1,4,32,1152]{3,2,1,0:T(8,128)(2,1)S(1)} %maximum_bitcast_fusion.5), channel_id=1, source_target_pairs={{0,16},{8,24},{16,0},{24,8},{1,17},{9,25},{17,1},{25,9},{2,18},{10... | collective-permute-start | bytes 884744 | tf_op jit(solution)/shard_map/ppermute | solution.py:162
  372.5 12.3 %collective-permute-start.35 = (bf16[1,4,32,1152]{3,2,1,0:T(8,128)(2,1)S(1)}, bf16[1,4,32,1152]{3,2,1,0:T(8,128)(2,1)S(1)}, u32[]{:S(2)}, u32[]{:S(2)}) collective-permute-start(bf16[1,4,32,1152]{3,2,1,0:T(8,128)(2,1)S(1)} %maximum_bitcast_fusion.3), channel_id=1, source_target_pairs={{0,16},{8,24},{16,0},{24,8},{1,17},{9,25},{17,1},{25,9},{2,18},{10... | collective-permute-start | bytes 884744 | tf_op jit(solution)/shard_map/ppermute | solution.py:162
  378.5 7.5 %collective-permute-start.42 = (bf16[2,4,32,1152]{3,2,1,0:T(8,128)(2,1)S(1)}, bf16[2,4,32,1152]{3,2,1,0:T(8,128)(2,1)S(1)}, u32[]{:S(2)}, u32[]{:S(2)}) collective-permute-start(bf16[2,4,32,1152]{3,2,1,0:T(8,128)(2,1)S(1)} %pad_maximum_fusion.7), channel_id=1, source_target_pairs={{0,8},{8,0},{16,24},{24,16},{1,9},{9,1},{17,25},{25,17},{2,10},{10... | collective-permute-start | bytes 1769480 | tf_op jit(solution)/shard_map/ppermute | solution.py:162
  381.7 4.5 %collective-permute-start.48 = (bf16[2,4,32,1152]{3,2,1,0:T(8,128)(2,1)S(1)}, bf16[2,4,32,1152]{3,2,1,0:T(8,128)(2,1)S(1)}, u32[]{:S(2)}, u32[]{:S(2)}) collective-permute-start(bf16[2,4,32,1152]{3,2,1,0:T(8,128)(2,1)S(1)} %pad_maximum_fusion.8), channel_id=1, source_target_pairs={{0,8},{8,0},{16,24},{24,16},{1,9},{9,1},{17,25},{25,17},{2,10},{10... | collective-permute-start | bytes 1769480 | tf_op jit(solution)/shard_map/ppermute | solution.py:162
  384.9 2.1 collective-permute-start.36
  (19 other events, 66.8 us)
